TPU v7x, 128 devices: a whole 4x4x4 slice. The times are simulated.
128 devices in a mesh: fsdp: 16 (over x_hi, y, core), loop: 8 (over z, x_lo).
Axes of the slice: x: 4 (x_hi: 2, x_lo: 2; x = x_hi * 2 + x_lo), y: 4, z: 4, core: 2. Of those that a mesh axis runs over, the one named last changes fastest.
Arguments:
- iterate: bfloat16 [8, 7168, 2048], P(None, 'fsdp', 'loop'), may hold values from -0.0625 to 0.0625
- expert_order: int32 [8], replicated, may hold values from 0 to 7, each once
Outputs:
- update: bfloat16 [8, 7168, 2048], P(None, 'fsdp', 'loop')
Inputs may be any that keep to these rules, and one draw needn't show every extreme that they name: `expert_order`: each value names a different expert.
All inputs are finite; a program needn't handle non-finite values.
Results may differ from a plain program's by a relative error of at most 0.006.
Values may be sent and summed in bfloat16 or wider, within the bound.
A program may use at most 128 MiB of HBM per device.

v0:
```python
import jax
import jax.numpy as jnp
from jax import lax
from jax.sharding import PartitionSpec as P

D = 7168


coef_linear = 3.4445
coef_cubic = -4.775


def half_step(left, right):
    factor = 0.2 * D**0.5
    partial_gram = jnp.einsum("eic,eik->eck", left, right, preferred_element_type=jnp.float32)
    summed = lax.psum(partial_gram, "fsdp")
    gram_block = summed.astype(jnp.bfloat16)
    product = jnp.einsum("eik,eck->eic", right, gram_block, preferred_element_type=jnp.float32)
    result = factor * (coef_linear * left.astype(jnp.float32) + coef_cubic * product)
    return result.astype(jnp.bfloat16)


def body(iterate, expert_order):
    chosen = jnp.take(iterate, expert_order, axis=0)
    gathered = lax.all_gather(chosen, "loop", axis=2, tiled=True)
    return half_step(chosen, gathered)


def solution(mesh):
    placed = (P(None, "fsdp", "loop"), P())
    return jax.shard_map(
        body, mesh=mesh, in_specs=placed, out_specs=P(None, "fsdp", "loop"), check_vma=False
    )
```

profile of v0, /device:TPU:5, one launch (start us, length us, event | category | flops | bytes accessed | tf_op | source)
XLA Modules:
  0.0 525.6 jit_solution(17105883795488496706)
XLA Ops:
  6.5 0.0 copy-start
  6.5 0.0 all-gather.2.cloned.1.call-start
  6.5 0.8 compare_and_fusion
  7.3 0.7 compare_select_fusion
  8.0 0.0 copy-done
  8.1 1.9 gather_fusion
  9.9 3.0 broadcast_select_fusion
  12.9 0.0 all-gather.2.cloned.1.call-update
  12.9 288.2 %all-gather.2.cloned.1.call-done = bf16[8,448,2048]{2,1,0:T(8,128)(2,1)} async-done(((bf16[8,448,256]{2,1,0:T(8,128)(2,1)}), bf16[8,448,2048]{2,1,0:T(8,128)(2,1)}) %all-gather.2.cloned.1.call-update) | async-done | bytes 14680080 | tf_op jit(solution)/shard_map/all_gather | solution.py:25
  301.1 16.0 %fusion.4 = f32[8,256,2048]{2,1,0:T(8,128)} fusion(bf16[8,448,256]{2,1,0:T(8,128)(2,1)} %broadcast_select_fusion, bf16[8,448,2048]{2,1,0:T(8,128)(2,1)} %all-gather.2.cloned.1.call-done), kind=kOutput, calls=%fused_computation.8 | convolution fusion | flops 3758096384 | bytes 33292288 | tf_op jit(solution)/shard_map/eic,eik->eck/dot_general | solution.py:15
  317.2 189.1 %all-reduce.1 = bf16[8,256,2048]{2,1,0:T(8,128)(2,1)} all-reduce(f32[8,256,2048]{2,1,0:T(8,128)} %fusion.4), channel_id=1, replica_groups=mesh['fsdp'=16,'loop'=8] {'fsdp'}, use_global_device_ids=true, to_apply=%region_0.1 | all-reduce | flops 4194304 | bytes 25165824 | tf_op jit(solution)/shard_map/psum | solution.py:16
  506.3 12.5 %multiply_convert_fusion = bf16[8,448,256]{2,1,0:T(8,128)(2,1)} fusion(bf16[8,448,256]{2,1,0:T(8,128)(2,1)} %broadcast_select_fusion, bf16[8,448,2048]{2,1,0:T(8,128)(2,1)} %all-gather.2.cloned.1.call-done, bf16[8,256,2048]{2,1,0:T(8,128)(2,1)} %all-reduce.1), kind=kOutput, calls=%fused_computation.3 | convolution fusion | flops 3763601408 | bytes 26738688 | tf_op jit(solution)/shard_map/eik,eck->eic/dot_general | solution.py:18
  (1 shorter events, 0.0 us)
Async XLA Ops:
  6.5 1.5 copy-start
  6.5 294.6 %all-gather.2.cloned.1.call-start = ((), (), s32[]{:S(2)}) async-start(), calls=%async_computation | async-start | bytes 16515072 | tf_op jit(solution)/shard_map/all_gather | solution.py:25
Sparse Core Ops, SparseCore 0:
  13.1 288.0 all-gather.1
where the time goes:
time: 530 us; the launch traced here: 526 us
  waiting for transfers between devices  288 us (54%)
  blocking collectives  189 us (36%)
  matrix products  28.5 us (5%)
  between operations  13.4 us (3%)
    all_gather x1, waiting for transfers between devices, body(): gathered = lax.all_gather(chosen, 'loop', axis=2, tiled=True)  288 us
    psum x1, blocking collectives, half_step(): summed = lax.psum(partial_gram, 'fsdp')  189 us
    dot_general x1, matrix products, half_step(): jnp.einsum('eic,eik->eck', left, right, preferred_element_type=jnp.float32)  16 us
    dot_general x1, matrix products, half_step(): jnp.einsum('eik,eck->eic', right, gram_block, preferred_element_type=jnp....  12.5 us
  transfers between devices with their start and end apart: 1, of which 1 were waited for; matrix products, arithmetic and copies ran while one was open for 0% of the time, Pallas kernels for 0%

commit v1 on v0

v1 whole, which is shorter than its diff:
```python
import jax
import jax.numpy as jnp
from jax import lax
from jax.experimental import pallas as pl
from jax.experimental.pallas import tpu as pltpu
from jax.sharding import PartitionSpec as P

MESH = pl.DeviceIdType.MESH
D = 7168
coef_linear = 3.4445
coef_cubic = -4.775
FACTOR = 0.2 * D**0.5

EXPERTS = 8
ROWS = 448
COLS = 256
FF = 2048
SLABS = 4
SLAB = 2 * COLS
DZ = (0, 1, 3, 2)
WIDTH = tuple(SLAB * (s + 1) for s in range(SLABS))
BASE = tuple(SLAB * s * (s + 1) // 2 for s in range(SLABS))
TOTAL = BASE[-1] + WIDTH[-1]
BELOW = tuple(2 * COLS * sum(SLABS - 1 - u for u in range(s)) for s in range(SLABS))
SLICE = COLS // 8
BF16 = jnp.bfloat16
F32 = jnp.float32


def kernel(x_ref, o_ref, xe, xt, gpart, rbuf, grow, gcol, pbuf, local_sem, in_send, in_recv, fwd_send, fwd_recv,
           rs_send, rs_recv, ag_send, ag_recv, sib_send, sib_recv, out_send, out_recv):
    f, l = lax.axis_index("fsdp"), lax.axis_index("loop")
    core = lax.rem(f, 2)
    y = lax.rem(f // 2, 4)
    xh = f // 8
    z = l // 2
    xl = lax.rem(l, 2)
    flip = lambda bit: 1 - bit
    xor = lambda a, b: a + b - 2 * a * b
    mine = z * 2 + xor(xl, xh)
    e_lo = xor(xl, xh)
    q_me = xh * 4 + y
    sibling = (f + 1 - 2 * core, l)

    def plane(dz, x, c):
        return ((xh * 4 + y) * 2 + c, lax.rem(z + dz, 4) * 2 + x)

    def member(k):
        qx = xor(xh, k // 4)
        qy = lax.rem(y + lax.rem(k, 4), 4)
        return qx * 4 + qy, ((qx * 4 + qy) * 2 + core, z * 2 + xor(e_lo, qx))

    my_rows = pl.ds(pl.multiple_of(core * ROWS, ROWS), ROWS)
    block = lambda s, x: pl.ds(pl.multiple_of((2 * s + x) * COLS, COLS), COLS)

    barrier = pltpu.get_barrier_semaphore()

    def greet(device):
        pl.semaphore_signal(barrier, inc=1, device_id=device, device_id_type=MESH)

    for dz in range(4):
        for dx in range(2):
            for dc in range(2):
                if dz or dx or dc:
                    greet(plane(dz, xor(xl, dx), xor(core, dc)))
    for k in range(1, 8):
        greet(member(k)[1])
    own = pltpu.make_async_copy(x_ref.at[mine], xe.at[my_rows, block(0, xl)], local_sem.at[0])
    own.start()
    pl.semaphore_wait(barrier, 22)

    def in_copy(s, dx):
        back = (4 - DZ[s]) % 4
        x = xor(xl, dx)
        expert = lax.rem(z + back, 4) * 2 + xor(x, xh)
        return pltpu.make_async_remote_copy(
            x_ref.at[expert], xe.at[my_rows, block(s, xl)], in_send.at[s, dx], in_recv.at[s, dx],
            device_id=plane(back, x, core), device_id_type=MESH)

    def in_wait(s, dx):
        there = xe.at[my_rows, block(s, xor(xl, dx))]
        pltpu.make_async_remote_copy(there, there, in_send.at[s, dx], in_recv.at[s, dx], device_id=sibling,
                                     device_id_type=MESH).wait_recv()

    def forward(s, dx):
        there = xe.at[my_rows, block(s, xor(xl, dx))]
        return pltpu.make_async_remote_copy(there, there, fwd_send.at[s, dx], fwd_recv.at[s, dx], device_id=sibling,
                                            device_id_type=MESH)

    def forward_wait(s, dx):
        other = pl.ds(pl.multiple_of((1 - core) * ROWS, ROWS), ROWS)
        there = xe.at[other, block(s, xor(xl, dx))]
        pltpu.make_async_remote_copy(there, there, fwd_send.at[s, dx], fwd_recv.at[s, dx], device_id=sibling,
                                     device_id_type=MESH).wait_recv()

    for s in range(SLABS):
        for dx in range(2):
            if s or dx:
                in_copy(s, dx).start()
    own.wait()
    forward(0, 0).start()

    def rs_copy(s, k):
        q, device = member(k)
        rows = pl.ds(pl.multiple_of(q * SLICE, SLICE), SLICE)
        cols = pl.ds(BASE[s], WIDTH[s])
        return pltpu.make_async_remote_copy(
            gpart.at[rows, cols], rbuf.at[q_me, :, cols], rs_send.at[s, q], rs_recv.at[s, q_me], device_id=device,
            device_id_type=MESH)

    def rs_wait(s, k):
        q, device = member(k)
        there = rbuf.at[q, :, pl.ds(BASE[s], WIDTH[s])]
        pltpu.make_async_remote_copy(there, there, rs_send.at[s, q], rs_recv.at[s, q], device_id=device,
                                     device_id_type=MESH).wait_recv()

    my_slice = pl.ds(pl.multiple_of(q_me * SLICE, SLICE), SLICE)

    def ag_copy(s, k):
        q, device = member(k)
        there = grow.at[my_slice, pl.ds(BASE[s], WIDTH[s])]
        return pltpu.make_async_remote_copy(there, there, ag_send.at[s, q], ag_recv.at[s, q_me], device_id=device,
                                            device_id_type=MESH)

    def ag_wait(s, k):
        q, device = member(k)
        there = grow.at[pl.ds(pl.multiple_of(q * SLICE, SLICE), SLICE), pl.ds(BASE[s], WIDTH[s])]
        pltpu.make_async_remote_copy(there, there, ag_send.at[s, q], ag_recv.at[s, q], device_id=device,
                                     device_id_type=MESH).wait_recv()

    def each_member(action):
        lax.fori_loop(1, 8, lambda k, _: (action(k), 0)[1], 0)

    for s in range(SLABS):
        for dx in range(2):
            if s or dx:
                in_wait(s, dx)
                forward(s, dx).start()
        for dx in range(2):
            forward_wait(s, dx)
        xt[...] = xe[:, block(s, core)].T

        def tiles(t, _):
            cols = pl.ds(pl.multiple_of(t * SLAB, SLAB), SLAB)
            product = jnp.dot(xt[...], xe[:, cols], preferred_element_type=F32)
            gpart[:, pl.ds(pl.multiple_of(BASE[s] + t * SLAB, SLAB), SLAB)] = product.astype(BF16)
            return 0

        lax.fori_loop(0, s + 1, tiles, 0)
        each_member(lambda k: rs_copy(s, k).start())

    for s in reversed(range(SLABS)):
        each_member(lambda k: rs_wait(s, k))

        def add(t, _):
            cols = pl.ds(pl.multiple_of(BASE[s] + t * SLAB, SLAB), SLAB)

            def term(k, total):
                return total + rbuf[member(k)[0], :, cols].astype(F32)

            total = lax.fori_loop(1, 8, term, gpart[my_slice, cols].astype(F32))
            grow[my_slice, cols] = total.astype(BF16)
            return 0

        lax.fori_loop(0, s + 1, add, 0)
        each_member(lambda k: ag_copy(s, k).start())

    def tile_at(s, t, x):
        return pl.ds(pl.multiple_of(BELOW[s] + ((t - s - 1) * 2 + x) * COLS, COLS), COLS)

    def gram_cols(s, t, x):
        return pl.ds(pl.multiple_of(BASE[t] + (2 * s + x) * COLS, COLS), COLS)

    def sib_copy(s, t):
        return pltpu.make_async_remote_copy(
            grow.at[:, gram_cols(s, t, 1 - core)], gcol.at[tile_at(s, t, core)], sib_send.at[s, t], sib_recv.at[s, t],
            device_id=sibling, device_id_type=MESH)

    def sib_wait(s, t):
        there = gcol.at[tile_at(s, t, 1 - core)]
        pltpu.make_async_remote_copy(there, there, sib_send.at[s, t], sib_recv.at[s, t], device_id=sibling,
                                     device_id_type=MESH).wait_recv()

    def out_copy(s, r):
        return pltpu.make_async_remote_copy(
            pbuf.at[s, r], o_ref.at[mine], out_send.at[s, r], out_recv.at[mine], device_id=plane(DZ[s], core, r),
            device_id_type=MESH)

    def out_wait(e):
        there = o_ref.at[e]
        pltpu.make_async_remote_copy(there, there, out_send.at[0, 0], out_recv.at[e], device_id=sibling,
                                     device_id_type=MESH).wait_recv()

    home = pltpu.make_async_copy(pbuf.at[0, core], o_ref.at[mine], local_sem.at[1])
    at_home = xl == core

    for s in reversed(range(SLABS)):
        each_member(lambda k: ag_wait(s, k))
        for u in range(s):
            sib_copy(u, s).start()
        for u in range(s):
            gcol[tile_at(u, s, core), :] = grow[:, gram_cols(u, s, core)]
        for t in range(s + 1, SLABS):
            sib_wait(s, t)

        def rows_of(r, _):
            rows = pl.ds(pl.multiple_of(r * ROWS, ROWS), ROWS)
            product = lax.dot_general(xe[rows, 0:WIDTH[s]], grow[:, BASE[s]:BASE[s] + WIDTH[s]],
                                      (((1,), (1,)), ((), ())), preferred_element_type=F32)
            if s < SLABS - 1:
                product += jnp.dot(xe[rows, WIDTH[s]:FF], gcol[BELOW[s]:BELOW[s] + FF - WIDTH[s], :],
                                   preferred_element_type=F32)
            left = xe[rows, block(s, core)].astype(F32)
            pbuf[s, r] = (FACTOR * (coef_linear * left + coef_cubic * product)).astype(BF16)
            return 0

        lax.fori_loop(0, 2, rows_of, 0)
        if s:
            for r in range(2):
                out_copy(s, r).start()
        else:
            @pl.when(at_home)
            def _():
                home.start()
                out_copy(0, 1 - core).start()

            @pl.when(jnp.logical_not(at_home))
            def _():
                for r in range(2):
                    out_copy(0, r).start()

    for s in range(SLABS):
        for dx in range(2):
            if s or dx:
                in_copy(s, dx).wait_send()
            forward(s, dx).wait_send()
        each_member(lambda k: rs_copy(s, k).wait_send())
        each_member(lambda k: ag_copy(s, k).wait_send())
        for u in range(s):
            sib_copy(u, s).wait_send()
        if s:
            for r in range(2):
                out_copy(s, r).wait_send()

    @pl.when(at_home)
    def _():
        home.wait()
        out_copy(0, 1 - core).wait_send()

    @pl.when(jnp.logical_not(at_home))
    def _():
        for r in range(2):
            out_copy(0, r).wait_send()

    for e in range(EXPERTS):
        @pl.when(jnp.logical_not(jnp.logical_and(at_home, mine == e)))
        def _():
            out_wait(e)


def exchange(iterate):
    dma = pltpu.SemaphoreType.DMA
    return pl.pallas_call(
        kernel,
        name="gram_step",
        out_shape=jax.ShapeDtypeStruct((EXPERTS, ROWS, COLS), BF16),
        in_specs=[pl.BlockSpec(memory_space=pl.ANY)],
        out_specs=pl.BlockSpec(memory_space=pl.ANY),
        scratch_shapes=[
            pltpu.VMEM((2 * ROWS, FF), BF16),
            pltpu.VMEM((COLS, 2 * ROWS), BF16),
            pltpu.VMEM((COLS, TOTAL), BF16),
            pltpu.VMEM((8, SLICE, TOTAL), BF16),
            pltpu.VMEM((COLS, TOTAL), BF16),
            pltpu.VMEM((12 * COLS, COLS), BF16),
            pltpu.VMEM((SLABS, 2, ROWS, COLS), BF16),
            dma((2,)),
            dma((SLABS, 2)), dma((SLABS, 2)),
            dma((SLABS, 2)), dma((SLABS, 2)),
            dma((SLABS, 8)), dma((SLABS, 8)),
            dma((SLABS, 8)), dma((SLABS, 8)),
            dma((SLABS, SLABS)), dma((SLABS, SLABS)),
            dma((SLABS, 2)), dma((EXPERTS,)),
        ],
        compiler_params=pltpu.CompilerParams(collective_id=0, has_side_effects=True, vmem_limit_bytes=48 << 20),
    )(iterate)


def body(iterate, expert_order):
    return jnp.take(exchange(iterate), expert_order, axis=0)


def solution(mesh):
    placed = (P(None, "fsdp", "loop"), P())
    return jax.shard_map(
        body, mesh=mesh, in_specs=placed, out_specs=P(None, "fsdp", "loop"), check_vma=False
    )
```

time: 530 us -> 105 us (0.20)
  waiting for transfers between devices: 288 us -> 0 us
  blocking collectives: 189 us -> 0 us
  Pallas kernels: 0 us -> 98.3 us
  matrix products: 28.5 us -> 0 us
  between operations: 13.4 us -> 0.03 us
    all_gather x1 -> x0, waiting for transfers between devices: 288 us -> none  [body(): gathered = lax.all_gather(chosen, 'loop', axis=2, tiled=True)]
    psum x1 -> x0, blocking collectives: 189 us -> none  [half_step(): summed = lax.psum(partial_gram, 'fsdp')]
    pallas_call x0 -> x1, Pallas kernels: none -> 98.3 us  [exchange(): pl.pallas_call(kernel, name='gram_step', out_shape=jax.ShapeDtypeStruct((...]
    dot_general x2 -> x0, matrix products: 28.5 us -> none  [the longest x1 16 us: half_step(): jnp.einsum('eic,eik->eck', left, right, preferred_element_type=jnp.float32)]
  transfers between devices with their start and end apart: 1 -> 0, of which waited for: 1 -> 0; matrix products, arithmetic and copies ran while one was open for 0% -> 0% of each run, Pallas kernels for 0% -> 0%
where the time goes in v1:
time: 105 us
  Pallas kernels  98.3 us (94%)
  local copies, waits for them, and re-layouts  3.4 us (3%)
  other arithmetic  2.98 us (3%)
    pallas_call x1, Pallas kernels, exchange(): pl.pallas_call(kernel, name='gram_step', out_shape=jax.ShapeDtypeStruct((...  98.3 us
    select_n x2, other arithmetic, body(): return jnp.take(exchange(iterate), expert_order, axis=0)  2.97 us

profile of v1, /device:TPU:5, one launch (start us, length us, event | category | flops | bytes accessed | tf_op | source)
XLA Modules:
  0.0 104.7 jit_solution(10554785073205026938)
XLA Ops:
  0.0 0.0 copy-start
  0.0 1.5 %copy-done = bf16[8,448,256]{2,1,0:T(8,128)(2,1)S(1)} copy-done((bf16[8,448,256]{2,1,0:T(8,128)(2,1)S(1)}, bf16[8,448,256]{2,1,0:T(8,128)(2,1)}, u32[]{:S(2)}) %copy-start) | copy-done | bytes 1835032
  1.5 0.0 copy-start.1
  1.5 98.3 %gram_step.1 = bf16[8,448,256]{2,1,0:T(8,128)(2,1)S(1)} custom-call(bf16[8,448,256]{2,1,0:T(8,128)(2,1)S(1)} %copy-done), custom_call_target="tpu_custom_call" | custom-call | tf_op jit(solution)/shard_map/gram_step/pallas_call | solution.py:263
  99.8 0.0 copy-done.1
  99.8 1.9 %gather_fusion = bf16[8,448,256]{2,1,0:T(8,128)(2,1)} fusion(bf16[8,448,256]{2,1,0:T(8,128)(2,1)S(1)} %gram_step.1, s32[1024]{0:T(1024)S(1)} %pad_clamp_fusion), kind=kCustom, calls=%fused_computation | custom fusion | bytes 3670048 | tf_op jit(solution)/shard_map/jit(_take)/gather | solution.py:290
  101.7 3.0 %broadcast_select_fusion = bf16[8,448,256]{2,1,0:T(8,128)(2,1)} fusion(bf16[8,448,256]{2,1,0:T(8,128)(2,1)} %gather_fusion, pred[8]{0:T(512)(128)(4,1)S(1)} %compare_and_fusion), kind=kLoop, calls=%fused_computation.1 | loop fusion | flops 917504 | bytes 3670024 | tf_op jit(solution)/shard_map/jit(_take)/select_n | solution.py:290
  (3 shorter events, 0.0 us)
Async XLA Ops:
  0.0 1.5 %copy-start = (bf16[8,448,256]{2,1,0:T(8,128)(2,1)S(1)}, bf16[8,448,256]{2,1,0:T(8,128)(2,1)}, u32[]{:S(2)}) copy-start(bf16[8,448,256]{2,1,0:T(8,128)(2,1)} %x_ref.1) | copy-start | bytes 5505028
  1.5 98.3 %copy-start.1 = (s32[8]{0:T(128)S(1)}, s32[8]{0:T(128)}, u32[]{:S(2)}) copy-start(s32[8]{0:T(128)} %param.3) | copy-start | bytes 100

commit v2 on v0

v2 whole, which is shorter than its diff:
```python
import jax
import jax.numpy as jnp
from jax import lax
from jax.experimental import pallas as pl
from jax.experimental.pallas import tpu as pltpu
from jax.sharding import PartitionSpec as P

MESH = pl.DeviceIdType.MESH
coef_linear = 3.4445
coef_cubic = -4.775
FACTOR = 0.2 * 7168**0.5

EXPERTS = 8
ROWS = 448
COLS = 256
FF = 2048
SLABS = 4
SLAB = 2 * COLS
DZ = (0, 1, 3, 2)
WIDTH = tuple(SLAB * s + COLS + COLS * (s % 2) for s in range(SLABS))
BASE = tuple(sum(WIDTH[:s]) for s in range(SLABS))
TOTAL = sum(WIDTH)
UPTO = tuple(SLAB * s + COLS for s in range(SLABS))
BELOW = tuple(sum(FF - UPTO[u] for u in range(s)) for s in range(SLABS))
SLICE = COLS // 8
CHUNKS = ((0, 0, 256, ()), (1, 0, 1024, (0, 1)), (2, 512, 768, (1,)), (2, 0, 512, (0,)), (3, 512, 512, (1,)),
          (3, 1024, 1024, (2, 3)), (3, 0, 512, (0,)))
A, B, C, D, E, F, G = range(7)
HALF = tuple(c[2] // 2 for c in CHUNKS)
HALF_AT = tuple(sum(HALF[:n]) for n in range(len(CHUNKS)))
QUARTER = COLS // 2
BF16 = jnp.bfloat16
F32 = jnp.float32


def kernel(x_ref, o_ref, xe, xt, gpart, from_x, from_y, pair_from_y, pair_to_x, pair_kept, pair_from_x, grow, gcol, pbuf, local_sem, in_send, in_recv, fwd_send, fwd_recv,
           rs_send, rs_recv, ag_send, ag_recv, sib_send, sib_recv, out_send, out_recv):
    f, l = lax.axis_index("fsdp"), lax.axis_index("loop")
    core = lax.rem(f, 2)
    y = lax.rem(f // 2, 4)
    xh = f // 8
    z = l // 2
    xl = lax.rem(l, 2)
    xor = lambda a, b: a + b - 2 * a * b
    e_lo = xor(xl, xh)
    mine = z * 2 + e_lo
    q_me = xh * 4 + y
    sibling = (f + 1 - 2 * core, l)

    def plane(dz, x, c):
        return ((xh * 4 + y) * 2 + c, lax.rem(z + dz, 4) * 2 + x)

    def member(qx, qy):
        return ((qx * 4 + qy) * 2 + core, z * 2 + xor(e_lo, qx))

    def remote(src, dst, send, recv, device):
        return pltpu.make_async_remote_copy(src, dst, send, recv, device_id=device, device_id_type=MESH)

    def arrived(there, recv):
        remote(there, there, recv, recv, sibling).wait_recv()

    my_rows = pl.ds(pl.multiple_of(core * ROWS, ROWS), ROWS)
    other_rows = pl.ds(pl.multiple_of((1 - core) * ROWS, ROWS), ROWS)
    block = lambda s, pos: pl.ds(pl.multiple_of((2 * s + pos) * COLS, COLS), COLS)

    barrier = pltpu.get_barrier_semaphore()

    def greet(device):
        pl.semaphore_signal(barrier, inc=1, device_id=device, device_id_type=MESH)

    def other_member(k):
        qx = xor(xh, k // 4)
        qy = lax.rem(y + k % 4, 4)
        return qx * 4 + qy, member(qx, qy)

    def each_member(action):
        for k in (4, 1, 3, 5, 7, 2, 6):
            action(k)

    for dz in range(4):
        for dx in range(2):
            for dc in range(2):
                if dz or dx or dc:
                    greet(plane(dz, xor(xl, dx), xor(core, dc)))
    each_member(lambda k: greet(other_member(k)[1]))
    pos_of = lambda dx: xor(xor(xl, dx), core)
    own = pltpu.make_async_copy(x_ref.at[mine], xe.at[my_rows, block(0, pos_of(0))], local_sem.at[0])
    own.start()
    pl.semaphore_wait(barrier, 22)

    def in_copy(s, dx):
        back = (4 - DZ[s]) % 4
        x = xor(xl, dx)
        expert = lax.rem(z + back, 4) * 2 + xor(x, xh)
        return remote(x_ref.at[expert], xe.at[my_rows, block(s, pos_of(0))], in_send, in_recv.at[s, dx],
                      plane(back, x, core))

    def in_wait(s, dx):
        arrived(xe.at[my_rows, block(s, pos_of(dx))], in_recv.at[s, dx])

    def forward(s, dx):
        return remote(xe.at[my_rows, block(s, pos_of(dx))], xe.at[my_rows, block(s, 1 - pos_of(dx))],
                      fwd_send, fwd_recv.at[s], sibling)

    for s in range(SLABS):
        for dx in range(2):
            if s or dx:
                in_copy(s, dx).start()
    own.wait()
    forward(0, 0).start()

    across = member(1 - xh, y)

    def along_y(action):
        for k in (1, 3, 2):
            action(lax.rem(y + k, 4))

    def columns(n):
        return pl.ds(BASE[CHUNKS[n][0]] + CHUNKS[n][1], CHUNKS[n][2])

    def halves(n):
        first, half = columns(n).start, HALF[n]
        return pl.ds(first, half), pl.ds(first + half, half), pl.ds(HALF_AT[n], half)

    def rows_of_y(w):
        return pl.ds(pl.multiple_of(w * SLICE, SLICE), SLICE)

    def rs_start(n):
        left, right, at = halves(n)
        remote(gpart.at[1 - xh, :, left], from_x.at[:, at], rs_send, rs_recv.at[n, 0], across).start()
        along_y(lambda w: remote(gpart.at[:, rows_of_y(w), right], pair_from_y.at[y, :, :, at], rs_send,
                                 rs_recv.at[n, 1], member(xh, w)).start())

    def by_columns(n, action):
        left, right, at = halves(n)

        def some(t, _):
            here = lambda base: pl.ds(pl.multiple_of(base + t * QUARTER, QUARTER), QUARTER)
            action(here(left.start), here(right.start), here(at.start))
            return 0

        lax.fori_loop(0, HALF[n] // QUARTER, some, 0)

    def middle(n):
        left, right, at = halves(n)
        arrived(from_x.at[:, at], rs_recv.at[n, 0])

        def over_x(lc, rc, c):
            gpart[xh, :, lc] = (gpart[xh, :, lc].astype(F32) + from_x[:, c].astype(F32)).astype(BF16)

        by_columns(n, over_x)
        along_y(lambda w: remote(gpart.at[xh, rows_of_y(w), left], from_y.at[y, :, at], rs_send, rs_recv.at[n, 2],
                                 member(xh, w)).start())
        arrived(pair_from_y.at[pl.ds(0, 3), :, :, at], rs_recv.at[n, 1])

        def over_y(lc, rc, c):
            for p in range(2):
                side = xh if p else 1 - xh
                total = gpart[side, rows_of_y(y), rc].astype(F32)
                for k in (1, 3, 2):
                    total += pair_from_y[lax.rem(y + k, 4), side, :, c].astype(F32)
                if p:
                    pair_kept[:, c] = total
                else:
                    pair_to_x[:, c] = total.astype(BF16)

        by_columns(n, over_y)
        remote(pair_to_x.at[:, at], pair_from_x.at[:, at], rs_send, rs_recv.at[n, 3], across).start()

    def slab(s):
        for dx in range(2):
            if s or dx:
                in_wait(s, dx)
                forward(s, dx).start()
        arrived(xe.at[other_rows, pl.ds(2 * s * COLS, SLAB)], fwd_recv.at[s])
        xt[s % 2] = xe[:, 2 * s * COLS:(2 * s + 1) * COLS].T

    def gram(n):
        s, first, width, _ = CHUNKS[n]
        end = min(first + width, UPTO[s])
        base = BASE[s]

        def tile(t, _):
            cols = pl.ds(pl.multiple_of(t * COLS, COLS), COLS)
            product = jnp.dot(xt[s % 2], xe[:, cols], preferred_element_type=F32)
            gpart[:, :, pl.ds(pl.multiple_of(base + t * COLS, COLS), COLS)] = product.astype(BF16).reshape(2, COLS // 2, COLS)
            return 0

        lax.fori_loop(first // COLS, end // COLS, tile, 0)
        if first + width > UPTO[s]:
            product = jnp.dot(xt[core], xe[:, block(s - 1 + core, 1)], preferred_element_type=F32)
            gpart[:, :, base + UPTO[s]:base + WIDTH[s]] = product.astype(BF16).reshape(2, COLS // 2, COLS)
        rs_start(n)

    my_slice = pl.ds(pl.multiple_of(q_me * SLICE, SLICE), SLICE)

    def piece(n, qx, qy, part):
        first, width = columns(n).start, CHUNKS[n][2]
        cols = (pl.ds(first, width), pl.ds(first, width // 2), pl.ds(first + width // 2, width // 2))[part]
        return grow.at[pl.ds(pl.multiple_of((qx * 4 + qy) * SLICE, SLICE), SLICE), cols]

    def add(n):
        left, right, at = halves(n)
        arrived(from_y.at[pl.ds(0, 3), :, at], rs_recv.at[n, 2])
        arrived(pair_from_x.at[:, at], rs_recv.at[n, 3])

        def final(lc, rc, c):
            total = gpart[xh, rows_of_y(y), lc].astype(F32)
            for k in (1, 3, 2):
                total += from_y[lax.rem(y + k, 4), :, c].astype(F32)
            grow[my_slice, lc] = total.astype(BF16)
            grow[my_slice, rc] = (pair_kept[:, c] + pair_from_x[:, c].astype(F32)).astype(BF16)

        by_columns(n, final)
        mine_full = piece(n, xh, y, 0)
        remote(mine_full, mine_full, ag_send, ag_recv.at[n, 1], across).start()
        along_y(lambda w: remote(mine_full, mine_full, ag_send, ag_recv.at[n, 0], member(xh, w)).start())

    def got(n, kind, rows):
        first, width = columns(n).start, CHUNKS[n][2]
        arrived(grow.at[pl.ds(0, rows), pl.ds(first, width if kind < 2 else width // 2)], ag_recv.at[n, kind])

    def pass_on(n):
        got(n, 0, 3 * SLICE)

        def over(w):
            part = piece(n, xh, w, 1)
            remote(part, part, ag_send, ag_recv.at[n, 2], across).start()

        along_y(over)
        got(n, 1, SLICE)
        part = piece(n, 1 - xh, y, 2)
        along_y(lambda w: remote(part, part, ag_send, ag_recv.at[n, 3], member(xh, w)).start())

    def complete(n):
        got(n, 2, 3 * SLICE)
        got(n, 3, 3 * SLICE)
        t = CHUNKS[n][0]
        for u in CHUNKS[n][3]:
            if u < t or t % 2:
                sib_copy(u, t).start()
        for u in CHUNKS[n][3]:
            if u < t:
                gcol[tile_at(u, t, 0), :] = grow[:, gram_cols(u, t, 0)]
            elif t % 2:
                gcol[pair_at(t), :] = grow[:, BASE[t] + UPTO[t]:BASE[t] + WIDTH[t]].T

    def tile_at(u, t, pos):
        return pl.ds(BELOW[u] + COLS + ((t - u - 1) * 2 + pos) * COLS, COLS)

    def gram_cols(u, t, pos):
        return pl.ds(BASE[t] + (2 * u + pos) * COLS, COLS)

    def sib_copy(u, t):
        if u < t:
            return remote(grow.at[:, gram_cols(u, t, 1)], gcol.at[tile_at(u, t, 1)], sib_send, sib_recv.at[u, t], sibling)
        return remote(grow.at[:, pl.ds(BASE[t] + UPTO[t], COLS)], gcol.at[pair_at(t)], sib_send, sib_recv.at[t, t], sibling)

    def pair_at(t):
        return pl.ds(pl.multiple_of(BELOW[t - 1] + core * (BELOW[t] - BELOW[t - 1]), COLS), COLS)

    def out_copy(s, r):
        return remote(pbuf.at[2 * s + r], o_ref.at[mine], out_send, out_recv, plane(DZ[s], core, r))

    home = pltpu.make_async_copy(pbuf.at[core], o_ref.at[mine], local_sem.at[1])
    at_home = xl == core

    def product_of(s, first_of_pair=False):
        if first_of_pair:
            arrived(gcol.at[pl.ds(0, COLS)], sib_recv.at[s | 1, s | 1])
        for t in range(s + 1, SLABS):
            arrived(gcol.at[tile_at(s, t, 1)], sib_recv.at[s, t])

        def rows_of(r, _):
            rows = pl.ds(pl.multiple_of(r * ROWS, ROWS), ROWS)
            product = lax.dot_general(xe[rows, 0:UPTO[s]], grow[:, BASE[s]:BASE[s] + UPTO[s]],
                                      (((1,), (1,)), ((), ())), preferred_element_type=F32)
            product += jnp.dot(xe[rows, UPTO[s]:FF], gcol[BELOW[s]:BELOW[s] + FF - UPTO[s], :],
                               preferred_element_type=F32)
            left = xe[rows, 2 * s * COLS:(2 * s + 1) * COLS].astype(F32)
            pbuf[2 * s + r] = (FACTOR * (coef_linear * left + coef_cubic * product)).astype(BF16)
            if s:
                out_copy(s, r).start()
            else:
                stays = jnp.logical_and(at_home, r == core)

                @pl.when(stays)
                def _():
                    home.start()

                @pl.when(jnp.logical_not(stays))
                def _():
                    out_copy(s, r).start()
            return 0

        lax.fori_loop(0, 2, rows_of, 0)

    slab(0)
    gram(A)
    slab(1)
    gram(B)
    middle(A)
    slab(2)
    gram(C)
    add(A)
    gram(D)
    middle(B)
    slab(3)
    gram(F)
    gram(E)
    gram(G)
    middle(C)
    middle(D)
    middle(F)
    middle(E)
    middle(G)
    add(F)
    add(E)
    add(G)
    add(B)
    pass_on(F)
    pass_on(E)
    pass_on(G)
    add(C)
    add(D)
    complete(F)
    complete(E)
    complete(G)
    product_of(3, first_of_pair=True)
    pass_on(B)
    pass_on(C)
    pass_on(D)
    complete(B)
    complete(C)
    product_of(1, first_of_pair=True)
    complete(D)
    product_of(2, first_of_pair=False)
    pass_on(A)
    complete(A)
    product_of(0, first_of_pair=False)

    def sent(there, send):
        remote(there, there, send, send, sibling).wait_send()

    sent(x_ref.at[pl.ds(0, 7)], in_send)
    sent(xe.at[pl.ds(0, ROWS)], fwd_send)
    sent(grow.at[pl.ds(0, 7 * SLICE)], rs_send)
    sent(grow.at[pl.ds(0, 7 * SLICE)], ag_send)
    sent(gcol.at[pl.ds(0, 8 * COLS)], sib_send)

    @pl.when(at_home)
    def _():
        home.wait()
        sent(pbuf.at[pl.ds(0, 7)], out_send)
        arrived(o_ref.at[pl.ds(0, 7)], out_recv)

    @pl.when(jnp.logical_not(at_home))
    def _():
        sent(pbuf, out_send)
        arrived(o_ref, out_recv)


def exchange(iterate):
    dma = pltpu.SemaphoreType.DMA
    return pl.pallas_call(
        kernel,
        name="gram_step",
        out_shape=jax.ShapeDtypeStruct((EXPERTS, ROWS, COLS), BF16),
        in_specs=[pl.BlockSpec(memory_space=pltpu.HBM)],
        out_specs=pl.BlockSpec(memory_space=pl.ANY),
        scratch_shapes=[
            pltpu.VMEM((2 * ROWS, FF), BF16),
            pltpu.VMEM((2, COLS, 2 * ROWS), BF16),
            pltpu.VMEM((2, COLS // 2, TOTAL), BF16),
            pltpu.VMEM((COLS // 2, TOTAL // 2), BF16),
            pltpu.VMEM((4, SLICE, TOTAL // 2), BF16),
            pltpu.VMEM((4, 2, SLICE, TOTAL // 2), BF16),
            pltpu.VMEM((SLICE, TOTAL // 2), BF16),
            pltpu.VMEM((SLICE, TOTAL // 2), F32),
            pltpu.VMEM((SLICE, TOTAL // 2), BF16),
            pltpu.VMEM((COLS, TOTAL), BF16),
            pltpu.VMEM((sum(FF - u for u in UPTO), COLS), BF16),
            pltpu.VMEM((2 * SLABS, ROWS, COLS), BF16),
            dma((2,)),
            dma, dma((SLABS, 2)),
            dma, dma((SLABS,)),
            dma, dma((len(CHUNKS), 4)),
            dma, dma((len(CHUNKS), 4)),
            dma, dma((SLABS, SLABS)),
            dma, dma,
        ],
        compiler_params=pltpu.CompilerParams(collective_id=0, has_side_effects=True, vmem_limit_bytes=51 << 20),
    )(iterate)


def body(iterate, expert_order):
    return exchange(iterate).at[expert_order].get(mode="promise_in_bounds")


def solution(mesh):
    placed = (P(None, "fsdp", "loop"), P())
    return jax.shard_map(
        body, mesh=mesh, in_specs=placed, out_specs=P(None, "fsdp", "loop"), check_vma=False
    )
```

time: 530 us -> 91.9 us (0.17)
  waiting for transfers between devices: 288 us -> 0 us
  blocking collectives: 189 us -> 0 us
  Pallas kernels: 0 us -> 89.2 us
  matrix products: 28.5 us -> 0 us
  between operations: 13.4 us -> 0.01 us
    all_gather x1 -> x0, waiting for transfers between devices: 288 us -> none  [body(): gathered = lax.all_gather(chosen, 'loop', axis=2, tiled=True)]
    psum x1 -> x0, blocking collectives: 189 us -> none  [half_step(): summed = lax.psum(partial_gram, 'fsdp')]
    pallas_call x0 -> x1, Pallas kernels: none -> 89.2 us  [exchange(): pl.pallas_call(kernel, name='gram_step', out_shape=jax.ShapeDtypeStruct((...]
    dot_general x2 -> x0, matrix products: 28.5 us -> none  [the longest x1 16 us: half_step(): jnp.einsum('eic,eik->eck', left, right, preferred_element_type=jnp.float32)]
  transfers between devices with their start and end apart: 1 -> 0, of which waited for: 1 -> 0; matrix products, arithmetic and copies ran while one was open for 0% -> 0% of each run, Pallas kernels for 0% -> 0%
where the time goes in v2:
time: 91.9 us; the launch traced here: 91.8 us
  Pallas kernels  89.2 us (97%)
  local copies, waits for them, and re-layouts  1.89 us (2%)
    pallas_call x1, Pallas kernels, exchange(): pl.pallas_call(kernel, name='gram_step', out_shape=jax.ShapeDtypeStruct((...  89.2 us
    gather x1, local copies, waits for them, and re-layouts, body(): return exchange(iterate).at[expert_order].get(mode='promise_in_bounds')  1.89 us

profile of v2, /device:TPU:5, one launch (start us, length us, event | category | flops | bytes accessed | tf_op | source)
XLA Modules:
  0.0 91.8 jit_solution(11030536146371156477)
XLA Ops:
  0.0 0.7 compare_select_fusion
  0.7 89.2 %gram_step.1 = bf16[8,448,256]{2,1,0:T(8,128)(2,1)S(1)} custom-call(bf16[8,448,256]{2,1,0:T(8,128)(2,1)} %x_ref.1), custom_call_target="tpu_custom_call" | custom-call | tf_op jit(solution)/shard_map/gram_step/pallas_call | solution.py:365
  89.9 1.9 %gather_fusion = bf16[8,448,256]{2,1,0:T(8,128)(2,1)} fusion(bf16[8,448,256]{2,1,0:T(8,128)(2,1)S(1)} %gram_step.1, s32[1024]{0:T(1024)S(1)} %pad_clamp_fusion), kind=kCustom, calls=%fused_computation | custom fusion | bytes 3670048 | tf_op jit(solution)/shard_map/gather | solution.py:397
  (1 shorter events, 0.0 us)

commit v3 on v2

--- a/solution.py
+++ b/solution.py
@@ -77,9 +77,9 @@
         for k in (4, 1, 3, 5, 7, 2, 6):
             action(k)
 
-    for dz in range(4):
-        for dx in range(2):
-            for dc in range(2):
+    for dz in (2, 1, 3, 0):
+        for dx in (1, 0):
+            for dc in (1, 0):
                 if dz or dx or dc:
                     greet(plane(dz, xor(xl, dx), xor(core, dc)))
     each_member(lambda k: greet(other_member(k)[1]))
@@ -239,11 +239,14 @@
         for u in CHUNKS[n][3]:
             if u < t or t % 2:
                 sib_copy(u, t).start()
+        if t in CHUNKS[n][3] and t % 2:
+            gcol[pair_at(t), :] = grow[:, BASE[t] + UPTO[t]:BASE[t] + WIDTH[t]].T
+
+    def place(n):
+        t = CHUNKS[n][0]
         for u in CHUNKS[n][3]:
             if u < t:
                 gcol[tile_at(u, t, 0), :] = grow[:, gram_cols(u, t, 0)]
-            elif t % 2:
-                gcol[pair_at(t), :] = grow[:, BASE[t] + UPTO[t]:BASE[t] + WIDTH[t]].T
 
     def tile_at(u, t, pos):
         return pl.ds(BELOW[u] + COLS + ((t - u - 1) * 2 + pos) * COLS, COLS)
@@ -330,10 +333,16 @@
     pass_on(B)
     pass_on(C)
     pass_on(D)
+    place(E)
+    place(G)
+    place(F)
     complete(B)
+    place(B)
     complete(C)
+    place(C)
     product_of(1, first_of_pair=True)
     complete(D)
+    place(D)
     product_of(2, first_of_pair=False)
     pass_on(A)
     complete(A)
@@ -394,7 +403,8 @@
 
 
 def body(iterate, expert_order):
-    return exchange(iterate).at[expert_order].get(mode="promise_in_bounds")
+    slots = lax.GatherDimensionNumbers(offset_dims=(1, 2), collapsed_slice_dims=(0,), start_index_map=(0,))
+    return lax.gather(exchange(iterate), expert_order[:, None], slots, (1, ROWS, COLS), mode="promise_in_bounds")
 
 
 def solution(mesh):

time: 91.9 us -> 91.8 us (level)
  no operation moved by 1% of the time
where the time goes in v3:
time: 91.8 us; the launch traced here: 91.7 us
  Pallas kernels  89.2 us (97%)
  local copies, waits for them, and re-layouts  1.89 us (2%)
    pallas_call x1, Pallas kernels, exchange(): pl.pallas_call(kernel, name='gram_step', out_shape=jax.ShapeDtypeStruct((...  89.2 us
    gather x1, local copies, waits for them, and re-layouts, body(): lax.gather(exchange(iterate), expert_order[:, None], slots, (1, ROWS, COL...  1.89 us

profile of v3, /device:TPU:5, one launch (start us, length us, event | category | flops | bytes accessed | tf_op | source)
XLA Modules:
  0.0 91.7 jit_solution(13976775143026828378)
XLA Ops:
  0.0 0.7 pad_clamp_fusion
  0.7 89.2 %gram_step.1 = bf16[8,448,256]{2,1,0:T(8,128)(2,1)S(1)} custom-call(bf16[8,448,256]{2,1,0:T(8,128)(2,1)} %x_ref.1), custom_call_target="tpu_custom_call" | custom-call | tf_op jit(solution)/shard_map/gram_step/pallas_call | solution.py:374
  89.8 1.9 %gather_fusion = bf16[8,448,256]{2,1,0:T(8,128)(2,1)} fusion(bf16[8,448,256]{2,1,0:T(8,128)(2,1)S(1)} %gram_step.1, s32[1024]{0:T(1024)S(1)} %pad_clamp_fusion), kind=kCustom, calls=%fused_computation | custom fusion | bytes 3670048 | tf_op jit(solution)/shard_map/gather | solution.py:407

commit v4 on v3

--- a/solution.py
+++ b/solution.py
@@ -24,8 +24,8 @@
 BELOW = tuple(sum(FF - UPTO[u] for u in range(s)) for s in range(SLABS))
 SLICE = COLS // 8
 CHUNKS = ((0, 0, 256, ()), (1, 0, 1024, (0, 1)), (2, 512, 768, (1,)), (2, 0, 512, (0,)), (3, 512, 512, (1,)),
-          (3, 1024, 1024, (2, 3)), (3, 0, 512, (0,)))
-A, B, C, D, E, F, G = range(7)
+          (3, 1024, 512, (2,)), (3, 0, 512, (0,)), (3, 1536, 512, (3,)))
+A, B, C, D, E, F, G, H = range(8)
 HALF = tuple(c[2] // 2 for c in CHUNKS)
 HALF_AT = tuple(sum(HALF[:n]) for n in range(len(CHUNKS)))
 QUARTER = COLS // 2
@@ -309,23 +309,28 @@
     gram(D)
     middle(B)
     slab(3)
+    gram(H)
     gram(F)
     gram(E)
     gram(G)
     middle(C)
     middle(D)
+    middle(H)
     middle(F)
     middle(E)
     middle(G)
+    add(H)
     add(F)
     add(E)
     add(G)
     add(B)
+    pass_on(H)
     pass_on(F)
     pass_on(E)
     pass_on(G)
     add(C)
     add(D)
+    complete(H)
     complete(F)
     complete(E)
     complete(G)

time: 91.8 us -> 91.8 us (level)
  no operation moved by 1% of the time
where the time goes in v4:
time: 91.8 us; the launch traced here: 91.7 us
  Pallas kernels  89.1 us (97%)
  local copies, waits for them, and re-layouts  1.89 us (2%)
    pallas_call x1, Pallas kernels, exchange(): pl.pallas_call(kernel, name='gram_step', out_shape=jax.ShapeDtypeStruct((...  89.1 us
    gather x1, local copies, waits for them, and re-layouts, body(): lax.gather(exchange(iterate), expert_order[:, None], slots, (1, ROWS, COL...  1.89 us

profile of v4, /device:TPU:5, one launch (start us, length us, event | category | flops | bytes accessed | tf_op | source)
XLA Modules:
  0.0 91.7 jit_solution(18012860264837817785)
XLA Ops:
  0.0 0.7 pad_clamp_fusion
  0.7 89.1 %gram_step.1 = bf16[8,448,256]{2,1,0:T(8,128)(2,1)S(1)} custom-call(bf16[8,448,256]{2,1,0:T(8,128)(2,1)} %x_ref.1), custom_call_target="tpu_custom_call" | custom-call | tf_op jit(solution)/shard_map/gram_step/pallas_call | solution.py:379
  89.8 1.9 %gather_fusion = bf16[8,448,256]{2,1,0:T(8,128)(2,1)} fusion(bf16[8,448,256]{2,1,0:T(8,128)(2,1)S(1)} %gram_step.1, s32[1024]{0:T(1024)S(1)} %pad_clamp_fusion), kind=kCustom, calls=%fused_computation | custom fusion | bytes 3670048 | tf_op jit(solution)/shard_map/gather | solution.py:412

commit v5 on v4

--- a/solution.py
+++ b/solution.py
@@ -214,23 +214,28 @@
         by_columns(n, final)
         mine_full = piece(n, xh, y, 0)
         remote(mine_full, mine_full, ag_send, ag_recv.at[n, 1], across).start()
-        along_y(lambda w: remote(mine_full, mine_full, ag_send, ag_recv.at[n, 0], member(xh, w)).start())
+        for step in (1, 3, 2):
+            kind = 4 if step == 2 else 0
+            remote(mine_full, mine_full, ag_send, ag_recv.at[n, kind], member(xh, lax.rem(y + step, 4))).start()
 
     def got(n, kind, rows):
         first, width = columns(n).start, CHUNKS[n][2]
-        arrived(grow.at[pl.ds(0, rows), pl.ds(first, width if kind < 2 else width // 2)], ag_recv.at[n, kind])
+        half = kind in (2, 3)
+        arrived(grow.at[pl.ds(0, rows), pl.ds(first, width // 2 if half else width)], ag_recv.at[n, kind])
 
     def pass_on(n):
-        got(n, 0, 3 * SLICE)
-
-        def over(w):
-            part = piece(n, xh, w, 1)
+        def over(step):
+            part = piece(n, xh, lax.rem(y + step, 4), 1)
             remote(part, part, ag_send, ag_recv.at[n, 2], across).start()
 
-        along_y(over)
+        got(n, 0, 2 * SLICE)
+        over(1)
+        over(3)
         got(n, 1, SLICE)
         part = piece(n, 1 - xh, y, 2)
         along_y(lambda w: remote(part, part, ag_send, ag_recv.at[n, 3], member(xh, w)).start())
+        got(n, 4, SLICE)
+        over(2)
 
     def complete(n):
         got(n, 2, 3 * SLICE)
@@ -399,7 +404,7 @@
             dma, dma((SLABS, 2)),
             dma, dma((SLABS,)),
             dma, dma((len(CHUNKS), 4)),
-            dma, dma((len(CHUNKS), 4)),
+            dma, dma((len(CHUNKS), 5)),
             dma, dma((SLABS, SLABS)),
             dma, dma,
         ],

time: 91.8 us -> 91.8 us (level)
  no operation moved by 1% of the time
where the time goes in v5:
time: 91.8 us; the launch traced here: 91.7 us
  Pallas kernels  89.2 us (97%)
  local copies, waits for them, and re-layouts  1.89 us (2%)
    pallas_call x1, Pallas kernels, exchange(): pl.pallas_call(kernel, name='gram_step', out_shape=jax.ShapeDtypeStruct((...  89.2 us
    gather x1, local copies, waits for them, and re-layouts, body(): lax.gather(exchange(iterate), expert_order[:, None], slots, (1, ROWS, COL...  1.89 us

profile of v5, /device:TPU:5, one launch (start us, length us, event | category | flops | bytes accessed | tf_op | source)
XLA Modules:
  0.0 91.7 jit_solution(10010014287856372594)
XLA Ops:
  0.0 0.7 pad_clamp_fusion
  0.7 89.2 %gram_step.1 = bf16[8,448,256]{2,1,0:T(8,128)(2,1)S(1)} custom-call(bf16[8,448,256]{2,1,0:T(8,128)(2,1)} %x_ref.1), custom_call_target="tpu_custom_call" | custom-call | tf_op jit(solution)/shard_map/gram_step/pallas_call | solution.py:384
  89.8 1.9 %gather_fusion = bf16[8,448,256]{2,1,0:T(8,128)(2,1)} fusion(bf16[8,448,256]{2,1,0:T(8,128)(2,1)S(1)} %gram_step.1, s32[1024]{0:T(1024)S(1)} %pad_clamp_fusion), kind=kCustom, calls=%fused_computation | custom fusion | bytes 3670048 | tf_op jit(solution)/shard_map/gather | solution.py:417

commit v6 on v4

--- a/solution.py
+++ b/solution.py
@@ -23,9 +23,9 @@
 UPTO = tuple(SLAB * s + COLS for s in range(SLABS))
 BELOW = tuple(sum(FF - UPTO[u] for u in range(s)) for s in range(SLABS))
 SLICE = COLS // 8
-CHUNKS = ((0, 0, 256, ()), (1, 0, 1024, (0, 1)), (2, 512, 768, (1,)), (2, 0, 512, (0,)), (3, 512, 512, (1,)),
-          (3, 1024, 512, (2,)), (3, 0, 512, (0,)), (3, 1536, 512, (3,)))
-A, B, C, D, E, F, G, H = range(8)
+CHUNKS = ((0, 0, 256, ()), (1, 0, 512, (0,)), (2, 512, 768, (1,)), (2, 0, 512, (0,)), (3, 512, 512, (1,)),
+          (3, 1024, 512, (2,)), (3, 0, 512, (0,)), (3, 1536, 512, (3,)), (1, 512, 512, (1,)))
+A, B, C, D, E, F, G, H, I = range(9)
 HALF = tuple(c[2] // 2 for c in CHUNKS)
 HALF_AT = tuple(sum(HALF[:n]) for n in range(len(CHUNKS)))
 QUARTER = COLS // 2
@@ -302,12 +302,14 @@
     gram(A)
     slab(1)
     gram(B)
+    gram(I)
     middle(A)
     slab(2)
     gram(C)
     add(A)
     gram(D)
     middle(B)
+    middle(I)
     slab(3)
     gram(H)
     gram(F)
@@ -324,6 +326,7 @@
     add(E)
     add(G)
     add(B)
+    add(I)
     pass_on(H)
     pass_on(F)
     pass_on(E)
@@ -336,6 +339,7 @@
     complete(G)
     product_of(3, first_of_pair=True)
     pass_on(B)
+    pass_on(I)
     pass_on(C)
     pass_on(D)
     place(E)
@@ -343,6 +347,7 @@
     place(F)
     complete(B)
     place(B)
+    complete(I)
     complete(C)
     place(C)
     product_of(1, first_of_pair=True)

time: 91.8 us -> 91.8 us (level)
  no operation moved by 1% of the time
where the time goes in v6:
time: 91.8 us; the launch traced here: 91.7 us
  Pallas kernels  89.1 us (97%)
  local copies, waits for them, and re-layouts  1.89 us (2%)
    pallas_call x1, Pallas kernels, exchange(): pl.pallas_call(kernel, name='gram_step', out_shape=jax.ShapeDtypeStruct((...  89.1 us
    gather x1, local copies, waits for them, and re-layouts, body(): lax.gather(exchange(iterate), expert_order[:, None], slots, (1, ROWS, COL...  1.89 us

profile of v6, /device:TPU:5, one launch (start us, length us, event | category | flops | bytes accessed | tf_op | source)
XLA Modules:
  0.0 91.7 jit_solution(4180090366609720460)
XLA Ops:
  0.0 0.7 pad_clamp_fusion
  0.7 89.1 %gram_step.1 = bf16[8,448,256]{2,1,0:T(8,128)(2,1)S(1)} custom-call(bf16[8,448,256]{2,1,0:T(8,128)(2,1)} %x_ref.1), custom_call_target="tpu_custom_call" | custom-call | tf_op jit(solution)/shard_map/gram_step/pallas_call | solution.py:384
  89.8 1.9 %gather_fusion = bf16[8,448,256]{2,1,0:T(8,128)(2,1)} fusion(bf16[8,448,256]{2,1,0:T(8,128)(2,1)S(1)} %gram_step.1, s32[1024]{0:T(1024)S(1)} %pad_clamp_fusion), kind=kCustom, calls=%fused_computation | custom fusion | bytes 3670048 | tf_op jit(solution)/shard_map/gather | solution.py:417
